TPU v7x, 256 devices: a whole 4x4x8 slice. The times are simulated.
256 devices in a mesh: wide: 16 (over y_lo, z), row: 16 (over y_hi, x, core).
Axes of the slice: x: 4, y: 4 (y_hi: 2, y_lo: 2; y = y_hi * 2 + y_lo), z: 8, core: 2. Of those that a mesh axis runs over, the one named last changes fastest.
Arguments:
- hessian: float32 [18432, 18432], P('row', 'wide'), as said below
- weight: bfloat16 [4608, 18432], P('row', 'wide'), may hold values from -6 to 6
- pairs: int32 [2], replicated, may hold values from 0 to 47, as said below
Outputs:
- pruned_hessian: float32 [18432, 18432], P('row', 'wide')
- pruned_weight: bfloat16 [4608, 18432], P('row', 'wide')
Inputs may be any that keep to these rules, and one draw needn't show every extreme that they name: Two different head pairs, one of which is the last pair, 47. `hessian`: symmetric positive definite.
All inputs are finite; a program needn't handle non-finite values.
Results may differ from a plain program's by a relative error of at most 0.001.
Values may be sent and summed in bfloat16 or wider, within the bound.
A program may use at most 128 MiB of HBM per device.

v0:
```python
import jax
import jax.numpy as jnp
from jax import lax
from jax.sharding import PartitionSpec as P

HEAD = 192


def broadcast(value, axis, source):
    kept = jnp.where(lax.axis_index(axis) == source, value, 0).astype(value.dtype)
    return lax.psum(kept, axis)


def per_device(hessian, weight, pairs):
    tile_rows, tile_cols = hessian.shape
    pair_width = 2 * HEAD
    row_here = lax.axis_index("row")
    highest = lax.Precision.HIGHEST
    pair_one = pairs[0]
    pair_two = pairs[1]

    def where_is(pair_index, extent):
        start_col = pair_index * pair_width
        return (start_col // extent, start_col % extent)

    def column_panel(matrix, pair_index):
        holder, offset = where_is(pair_index, tile_cols)
        local_cols = lax.dynamic_slice_in_dim(matrix, offset, pair_width, 1)
        return broadcast(local_cols, "wide", holder)

    def solved_rows(matrix, panel, pair_index):
        holder, offset = where_is(pair_index, tile_rows)
        pivot_block = lax.dynamic_slice_in_dim(panel, offset, pair_width, 0)
        pivot_block = jnp.where(
            row_here == holder, pivot_block, jnp.eye(pair_width, dtype=jnp.float32)
        )
        rows_local = lax.dynamic_slice_in_dim(matrix, offset, pair_width, 0)
        factor = jnp.linalg.cholesky(pivot_block)
        solved = jax.scipy.linalg.cho_solve((factor, True), rows_local)
        return broadcast(solved, "row", holder)

    panel_one = column_panel(hessian, pair_one)
    solved_one = solved_rows(hessian, panel_one, pair_one)
    holder_one, offset_one = where_is(pair_one, tile_cols)
    weight_one = broadcast(
        lax.dynamic_slice_in_dim(weight, offset_one, pair_width, 1), "wide", holder_one
    )
    updated = hessian - jnp.dot(panel_one, solved_one, precision=highest)
    carried = weight.astype(jnp.float32) - jnp.dot(
        weight_one.astype(jnp.float32), solved_one, precision=highest
    )
    panel_two = column_panel(updated, pair_two)
    solved_two = solved_rows(updated, panel_two, pair_two)
    holder_two, offset_two = where_is(pair_two, tile_cols)
    weight_two = broadcast(
        lax.dynamic_slice_in_dim(carried, offset_two, pair_width, 1), "wide", holder_two
    )
    pruned_hessian = updated - jnp.dot(panel_two, solved_two, precision=highest)
    pruned_weight = (carried - jnp.dot(weight_two, solved_two, precision=highest)).astype(
        jnp.bfloat16
    )
    return (pruned_hessian, pruned_weight)


def solution(mesh):
    return jax.shard_map(
        per_device,
        mesh=mesh,
        in_specs=(P("row", "wide"), P("row", "wide"), P()),
        out_specs=(P("row", "wide"), P("row", "wide")),
        check_vma=False,
    )
```

profile of v0, /device:TPU:1, one launch (start us, length us, event | category | flops | bytes accessed | tf_op | source)
XLA Modules:
  0.0 914.4 jit_solution(16918178659369243016)
XLA Ops:
  7.2 1.3 fusion.59
  9.2 6.9 copy.7
  16.1 2.9 dynamic-slice_select_fusion.1
  19.0 1.8 dynamic-slice_select_fusion.3
  20.9 132.6 %all-reduce.8.cloned.1.call-done = f32[1152,384]{0,1:T(8,128)} async-done(((f32[1152,384]{0,1:T(8,128)}), f32[1152,384]{0,1:T(8,128)}) %all-reduce.8.cloned.1.call-update) | async-done | bytes 1769488 | tf_op jit(solution)/shard_map/psum | solution.py:11
  153.5 1.5 convert_select_fusion.1
  155.4 11.7 %cholesky.208 = f32[128,128]{1,0:T(8,128)S(1)} custom-call(f32[128,128]{1,0:T(8,128)S(1)} %cholesky.310), custom_call_target="Cholesky" | custom-call | tf_op jit(solution)/shard_map/jit(cholesky)/cholesky | solution.py:38
  167.2 9.8 %custom-call.22 = f32[1,128,128]{1,2,0:T(8,128)S(1)} custom-call(f32[1,128,128]{2,1,0:T(8,128)S(1)} %get-tuple-element.57), custom_call_target="InvertDiagBlocksLowerTriangular" | custom-call | tf_op jit(solution)/shard_map/jit(cholesky)/cholesky | solution.py:38
  177.6 11.7 %cholesky.227 = f32[128,128]{1,0:T(8,128)S(1)} custom-call(f32[128,128]{1,0:T(8,128)S(1)} %cholesky.314), custom_call_target="Cholesky" | custom-call | tf_op jit(solution)/shard_map/jit(cholesky)/cholesky | solution.py:38
  189.4 10.1 %custom-call.23 = f32[1,128,128]{1,2,0:T(8,128)S(1)} custom-call(f32[1,128,128]{2,1,0:T(8,128)S(1)} %get-tuple-element.54), custom_call_target="InvertDiagBlocksLowerTriangular" | custom-call | tf_op jit(solution)/shard_map/jit(cholesky)/cholesky | solution.py:38
  200.0 11.7 %cholesky.246 = f32[128,128]{1,0:T(8,128)S(1)} custom-call(f32[128,128]{1,0:T(8,128)S(1)} %convolution_subtract_fusion.15), custom_call_target="Cholesky" | custom-call | tf_op jit(solution)/shard_map/jit(cholesky)/cholesky | solution.py:38
  215.1 6.1 while.4
  215.8 1.3 bitcast_dynamic-update-slice_fusion.4
  217.8 1.3 bitcast_dynamic-update-slice_fusion.4
  219.9 1.3 bitcast_dynamic-update-slice_fusion.4
  221.2 29.5 %custom-call.24 = f32[3,128,128]{1,2,0:T(8,128)S(1)} custom-call(f32[3,128,128]{2,1,0:T(8,128)S(1)} %get-tuple-element.18), custom_call_target="InvertDiagBlocksLowerTriangular" | custom-call | tf_op jit(solution)/shard_map/jit(_cho_solve)/triangular_solve | solution.py:39
  250.7 1.8 fusion.15
  252.5 1.7 convolution_subtract_fusion.11
  254.9 1.9 convolution_subtract_fusion.10
  263.0 26.9 %all-reduce.14.cloned.1.call-done = bf16[288,384]{1,0:T(8,128)(2,1)} async-done(((bf16[288,384]{1,0:T(8,128)(2,1)}), bf16[288,384]{1,0:T(8,128)(2,1)}) %all-reduce.14.cloned.1.call-update) | async-done | bytes 221200 | tf_op jit(solution)/shard_map/psum | solution.py:11
  290.0 157.4 %all-reduce.10.cloned.1.call-done = f32[384,1152]{1,0:T(8,128)} async-done(((f32[384,1152]{1,0:T(8,128)}), f32[384,1152]{1,0:T(8,128)}) %all-reduce.10.cloned.1.call-update) | async-done | bytes 1769488 | tf_op jit(solution)/shard_map/psum | solution.py:11
  447.4 3.2 convolution_subtract_fusion.2
  451.6 12.4 %convolution_subtract_fusion.1 = f32[1152,1152]{0,1:T(8,128)S(1)} fusion(f32[1152,1152]{0,1:T(8,128)} %copy.7, f32[1152,384]{0,1:T(8,128)S(1)} %copy-done.1, f32[384,1152]{1,0:T(8,128)S(1)} %copy-done.3), kind=kOutput, calls=%fused_computation.5 | convolution fusion | flops 6116622336 | bytes 14155776 | tf_op jit(solution)/shard_map/dot_general | solution.py:48
  464.0 2.4 copy-done
  466.4 1.4 dynamic-slice_select_fusion
  468.2 133.6 %all-reduce.16.cloned.1.call-done = (f32[1152,384]{0,1:T(8,128)}, f32[288,384]{1,0:T(8,128)}) async-done(((f32[1152,384]{0,1:T(8,128)}, f32[288,384]{1,0:T(8,128)}), (f32[1152,384]{0,1:T(8,128)}, f32[288,384]{1,0:T(8,128)})) %all-reduce.16.cloned.1.call-update) | async-done | bytes 2211856 | tf_op jit(solution)/shard_map/psum | solution.py:11
  601.8 2.2 convert_select_fusion
  604.0 2.1 copy.9
  608.3 11.7 %cholesky.261 = f32[128,128]{1,0:T(8,128)S(1)} custom-call(f32[128,128]{1,0:T(8,128)S(1)} %cholesky.318), custom_call_target="Cholesky" | custom-call | tf_op jit(solution)/shard_map/jit(cholesky)/cholesky | solution.py:38
  620.7 9.8 %custom-call.25 = f32[1,128,128]{1,2,0:T(8,128)S(1)} custom-call(f32[1,128,128]{2,1,0:T(8,128)S(1)} %get-tuple-element.50), custom_call_target="InvertDiagBlocksLowerTriangular" | custom-call | tf_op jit(solution)/shard_map/jit(cholesky)/cholesky | solution.py:38
  631.3 1.8 constant_dynamic-update-slice_fusion
  634.3 11.7 %cholesky.280 = f32[128,128]{1,0:T(8,128)S(1)} custom-call(f32[128,128]{1,0:T(8,128)S(1)} %cholesky.322), custom_call_target="Cholesky" | custom-call | tf_op jit(solution)/shard_map/jit(cholesky)/cholesky | solution.py:38
  647.4 9.9 %custom-call.26 = f32[1,128,128]{1,2,0:T(8,128)S(1)} custom-call(f32[1,128,128]{2,1,0:T(8,128)S(1)} %get-tuple-element.47), custom_call_target="InvertDiagBlocksLowerTriangular" | custom-call | tf_op jit(solution)/shard_map/jit(cholesky)/cholesky | solution.py:38
  659.4 11.7 %cholesky.299 = f32[128,128]{1,0:T(8,128)S(1)} custom-call(f32[128,128]{1,0:T(8,128)S(1)} %convolution_subtract_fusion.14), custom_call_target="Cholesky" | custom-call | tf_op jit(solution)/shard_map/jit(cholesky)/cholesky | solution.py:38
  674.4 1.9 select_select_fusion
  676.4 8.5 while.5
  677.1 2.2 bitcast_dynamic-update-slice_fusion.5
  679.9 2.2 bitcast_dynamic-update-slice_fusion.5
  682.8 2.1 bitcast_dynamic-update-slice_fusion.5
  684.9 29.5 %custom-call.27 = f32[3,128,128]{1,2,0:T(8,128)S(1)} custom-call(f32[3,128,128]{2,1,0:T(8,128)S(1)} %get-tuple-element.19), custom_call_target="InvertDiagBlocksLowerTriangular" | custom-call | tf_op jit(solution)/shard_map/jit(_cho_solve)/triangular_solve | solution.py:39
  714.4 2.2 fusion.13
  716.6 2.5 convolution_subtract_fusion.7
  719.9 3.1 convolution_subtract_fusion.6
  727.2 1.3 maximum_select_fusion.1
  728.5 156.2 %all-reduce.12.cloned.1.call-done = f32[384,1152]{1,0:T(8,128)} async-done(((f32[384,1152]{1,0:T(8,128)}), f32[384,1152]{1,0:T(8,128)}) %all-reduce.12.cloned.1.call-update) | async-done | bytes 1769488 | tf_op jit(solution)/shard_map/psum | solution.py:11
  884.7 12.7 %convolution_subtract_fusion = f32[1152,1152]{0,1:T(8,128)} fusion(f32[1152,1152]{0,1:T(8,128)} %copy-done, f32[1152,384]{0,1:T(8,128)S(1)} %copy-done.2, f32[384,1152]{1,0:T(8,128)} %all-reduce.12.cloned.1.call-done), kind=kOutput, calls=%fused_computation.4 | convolution fusion | flops 6116622336 | bytes 14155776 | tf_op jit(solution)/shard_map/dot_general | solution.py:58
  897.4 7.0 copy.11
  904.4 3.3 fusion
  (85 shorter events, 29.3 us)
Async XLA Ops:
  7.2 146.3 %all-reduce.8.cloned.1.call-start = ((), (), s32[]{:S(2)}) async-start(), calls=%async_computation | async-start | bytes 3538944 | tf_op jit(solution)/shard_map/psum | solution.py:11
  19.0 271.0 %all-reduce.14.cloned.1.call-start = ((), (), s32[]{:S(2)}) async-start(), calls=%async_computation.3 | async-start | bytes 442368 | tf_op jit(solution)/shard_map/psum | solution.py:11
  20.8 426.6 %all-reduce.10.cloned.1.call-start = ((), (), s32[]{:S(2)}) async-start(), calls=%async_computation.1 | async-start | bytes 3538944 | tf_op jit(solution)/shard_map/psum | solution.py:11
  153.5 1.7 copy-start.1
  262.2 339.6 %all-reduce.16.cloned.1.call-start = ((), (), s32[]{:S(2)}) async-start(), calls=%async_computation.4 | async-start | bytes 4423680 | tf_op jit(solution)/shard_map/psum | solution.py:11
  447.4 4.1 copy-start.3
  464.0 2.4 copy-start
  467.8 417.0 %all-reduce.12.cloned.1.call-start = ((), (), s32[]{:S(2)}) async-start(), calls=%async_computation.2 | async-start | bytes 3538944 | tf_op jit(solution)/shard_map/psum | solution.py:11
  601.8 4.4 copy-start.2
  607.5 0.8 copy-start.6
  716.6 3.3 copy-start.5
  897.4 7.0 copy-start.4
  897.4 7.0 copy-start.7
Sparse Core Ops, SparseCore 0:
  19.1 134.3 all-reduce.7
  156.6 133.2 all-reduce.13
  292.7 154.7 all-reduce.9
  467.9 133.8 all-reduce.15
  728.7 156.0 all-reduce.11
where the time goes:
time: 925 us; the launch traced here: 914 us
  waiting for transfers between devices  607 us (66%)
  other arithmetic  191 us (21%)
  matrix products  60.4 us (7%)
  local copies, waits for them, and re-layouts  36.2 us (4%)
  between operations  19.5 us (2%)
    psum x5, waiting for transfers between devices, broadcast(): return lax.psum(kept, axis)  607 us
    another operation x21, other arithmetic, solved_rows(): factor = jnp.linalg.cholesky(pivot_block)  115 us
    another operation x5, other arithmetic, solved_rows(): solved = jax.scipy.linalg.cho_solve((factor, True), rows_local)  61 us
    another operation x20, matrix products, solved_rows(): solved = jax.scipy.linalg.cho_solve((factor, True), rows_local)  22.8 us
  transfers between devices with their start and end apart: 5, of which 5 were waited for; matrix products, arithmetic and copies ran while one was open for 12% of the time, Pallas kernels for 0%

commit v1 on v0

v1 whole, which is shorter than its diff:
```python
import functools

import jax
import jax.numpy as jnp
from jax import lax
from jax.experimental import pallas as pl
from jax.experimental.pallas import tpu as pltpu
from jax.sharding import PartitionSpec as P

HEAD = 192
PAIR = 2 * HEAD
NPAIRS = 48
N = 16
LAST = N - 1
MESH = pl.DeviceIdType.MESH
F32 = jnp.float32
BF16 = jnp.bfloat16
ANY = pl.BlockSpec(memory_space=pl.ANY)
VM = pl.BlockSpec(memory_space=pltpu.VMEM)


def remote(src, dst, send, recv, where):
    return pltpu.make_async_remote_copy(
        src_ref=src, dst_ref=dst, send_sem=send, recv_sem=recv,
        device_id=where, device_id_type=MESH,
    )


def greet_groups():
    row, wide = lax.axis_index("row"), lax.axis_index("wide")
    barrier = pltpu.get_barrier_semaphore()

    def body(d, _):
        pl.semaphore_signal(
            barrier, inc=1, device_id={"row": lax.rem(row + d, N)}, device_id_type=MESH
        )
        pl.semaphore_signal(
            barrier, inc=1, device_id={"wide": lax.rem(wide + d, N)}, device_id_type=MESH
        )
        return 0

    lax.fori_loop(1, N, body, 0)
    pl.semaphore_wait(barrier, 2 * (N - 1))


def scatter_kernel(root, cq, wq, pq, rq, c7, w7, r7,
                   ocq, owq, orq, oc7, ow7, or7, opv, pst, ssem, rsem, lsem):
    row, wide = lax.axis_index("row"), lax.axis_index("wide")
    greet_groups()
    at_wide, at_row = wide == root, row == root
    last_wide, last_row = wide == LAST, row == LAST

    def corner(ref):
        return lambda m: ref.at[m, :, pl.ds(2 * PAIR, PAIR)]

    jobs = [
        (0, jnp.logical_and(at_row, at_wide), at_row, "wide", wide, lambda m: pq.at[m], pst.at[0]),
        (1, jnp.logical_and(at_row, last_wide), at_row, "wide", wide, corner(rq), pst.at[1]),
        (2, jnp.logical_and(last_row, last_wide), last_row, "wide", wide, corner(r7), pst.at[2]),
        (3, at_row, None, "row", row, lambda m: rq.at[m], orq),
        (4, last_row, None, "row", row, lambda m: r7.at[m], or7),
        (5, at_wide, None, "wide", wide, lambda m: cq.at[m], ocq),
        (6, last_wide, None, "wide", wide, lambda m: c7.at[m], oc7),
        (7, at_wide, None, "wide", wide, lambda m: wq.at[m], owq),
        (8, last_wide, None, "wide", wide, lambda m: w7.at[m], ow7),
    ]

    def spread(job, act):
        k, mine, _, axis, me, src, dst = job

        @pl.when(mine)
        def _():
            def body(m, _):
                @pl.when(m != me)
                def _():
                    copy = remote(src(m), dst, ssem.at[k, m], rsem.at[k], {axis: m})
                    copy.start() if act == "start" else copy.wait_send()

                @pl.when(m == me)
                def _():
                    copy = pltpu.make_async_copy(src(m), dst, lsem.at[k])
                    copy.start() if act == "start" else copy.wait()
                return 0

            lax.fori_loop(0, N, body, 0)

    def arrive(job):
        k, mine, group, axis, me, src, dst = job
        away = jnp.logical_not(mine)
        if group is not None:
            away = jnp.logical_and(away, group)

        @pl.when(away)
        def _():
            remote(src(0), dst, ssem.at[k, 0], rsem.at[k], {axis: 0}).wait_recv()

    for job in jobs:
        spread(job, "start")
    for job in jobs[:3]:
        arrive(job)
        spread(job, "drain")
    second = [(9, at_row, 0, 0, root), (10, at_row, 1, 0, root), (11, last_row, 2, 1, LAST)]

    def forward(item, act):
        k, mine, part, core, origin = item

        @pl.when(mine)
        def _():
            def body(h, _):
                m = 2 * h + core

                @pl.when(m != origin)
                def _():
                    copy = remote(pst.at[part], opv.at[part], ssem.at[k, m], rsem.at[k], {"row": m})
                    copy.start() if act == "start" else copy.wait_send()

                @pl.when(m == origin)
                def _():
                    copy = pltpu.make_async_copy(pst.at[part], opv.at[part], lsem.at[k])
                    copy.start() if act == "start" else copy.wait()
                return 0

            lax.fori_loop(0, N // 2, body, 0)

    for item in second:
        forward(item, "start")
    for item in second:
        k, mine, part, core, origin = item
        away = jnp.logical_and(jnp.logical_not(mine), lax.rem(row, 2) == core)

        @pl.when(away)
        def _():
            remote(pst.at[part], opv.at[part], ssem.at[k, 0], rsem.at[k], {"row": 0}).wait_recv()

    for job in jobs[3:]:
        arrive(job)
    for item in second:
        forward(item, "drain")
    for job in jobs[3:]:
        spread(job, "drain")


def piece(dtype, *shape):
    return jax.ShapeDtypeStruct(shape, dtype)


PIECES = [
    piece(BF16, 72, PAIR), piece(BF16, 18, PAIR), piece(F32, 24, 1152),
    piece(BF16, 72, PAIR), piece(BF16, 18, PAIR), piece(F32, 24, 1152),
    piece(F32, 3, 24, PAIR),
]


def scatter(root, *operands):
    outs = PIECES + [piece(F32, 3, 24, PAIR)]
    return pl.pallas_call(
        functools.partial(scatter_kernel, root),
        name=f"scatter_{root}",
        out_shape=outs,
        in_specs=[ANY] * 7,
        out_specs=[ANY] * 8,
        scratch_shapes=[
            pltpu.SemaphoreType.DMA((12, N)),
            pltpu.SemaphoreType.DMA((12,)),
            pltpu.SemaphoreType.DMA((12,)),
        ],
        compiler_params=pltpu.CompilerParams(collective_id=1 + root, has_side_effects=True),
    )(*operands)[:7]


def gather_kernel(cq, wq, rq, c7, w7, r7, pv,
                  gcq, gwq, grq, gc7, gw7, gr7, gpv, ssem, rsem, lsem, fsem, gsem):
    row, wide = lax.axis_index("row"), lax.axis_index("wide")
    core = lax.rem(row, 2)
    greet_groups()
    along_wide = [(0, cq, gcq), (1, c7, gc7), (2, wq, gwq), (3, w7, gw7)]
    along_row = [(4, rq, grq), (5, r7, gr7)]
    pivots = [(6, pv.at[0], gpv.at[0], 0), (7, pv.at[1], gpv.at[1], 0), (8, pv.at[2], gpv.at[2], 1)]

    def wide_copy(k, src, dst, d):
        return remote(src, dst.at[wide], ssem.at[k, d], rsem.at[k, d], {"wide": lax.rem(wide + d, N)})

    def wide_arrival(k, src, dst, d):
        return remote(src, dst.at[lax.rem(wide + N - d, N)], ssem.at[k, d], rsem.at[k, d],
                      {"wide": lax.rem(wide + d, N)})

    def row_copy(k, src, dst, d):
        return remote(src, dst.at[row], ssem.at[k, d], rsem.at[k, d], {"row": lax.rem(row + d, N)})

    def row_arrival(k, src, dst, d):
        return remote(src, dst.at[lax.rem(row + N - d, N)], ssem.at[k, d], rsem.at[k, d],
                      {"row": lax.rem(row + d, N)})

    def over(n, f):
        def body(d, _):
            f(d)
            return 0
        lax.fori_loop(1, n, body, 0)

    for k, src, dst, c in pivots:
        @pl.when(core == c)
        def _():
            pltpu.make_async_copy(src, dst.at[wide], lsem.at[k]).start()
            over(N, lambda d: wide_copy(k, src, dst, d).start())
    for k, src, dst in along_row:
        pltpu.make_async_copy(src, dst.at[row], lsem.at[k]).start()
        over(N // 2, lambda d: row_copy(k, src, dst, 2 * d).start())
    for k, src, dst in along_wide:
        pltpu.make_async_copy(src, dst.at[wide], lsem.at[k]).start()
        over(N, lambda d: wide_copy(k, src, dst, d).start())

    partner = {"row": row + 1 - 2 * core}
    for k, src, dst, c in pivots:
        @pl.when(core == c)
        def _():
            pltpu.make_async_copy(src, dst.at[wide], lsem.at[k]).wait()
            over(N, lambda d: wide_arrival(k, src, dst, d).wait_recv())
            remote(dst, dst, fsem.at[k - 6], gsem.at[k - 6], partner).start()
    for k, src, dst in along_row:
        pltpu.make_async_copy(src, dst.at[row], lsem.at[k]).wait()

    def relay(k, dst, d):
        block = dst.at[lax.rem(row + N - 2 * d, N)]
        return remote(block, block, fsem.at[3 + (k - 4) * 8 + d], gsem.at[3 + (k - 4) * 8 + d], partner)

    def relayed(k, dst, d):
        block = dst.at[lax.rem(row + 1 - 2 * core + N - 2 * d, N)]
        return remote(block, block, fsem.at[3 + (k - 4) * 8 + d], gsem.at[3 + (k - 4) * 8 + d], partner)

    for k, src, dst in along_row:
        relay(k, dst, 0).start()

        def step(d):
            row_arrival(k, src, dst, 2 * d).wait_recv()
            relay(k, dst, d).start()
        over(N // 2, step)
    for k, src, dst in along_wide:
        pltpu.make_async_copy(src, dst.at[wide], lsem.at[k]).wait()
        over(N, lambda d: wide_arrival(k, src, dst, d).wait_recv())
    for k, src, dst, c in pivots:
        @pl.when(core != c)
        def _():
            remote(dst, dst, fsem.at[k - 6], gsem.at[k - 6], partner).wait_recv()

        @pl.when(core == c)
        def _():
            remote(dst, dst, fsem.at[k - 6], gsem.at[k - 6], partner).wait_send()
            over(N, lambda d: wide_copy(k, src, dst, d).wait_send())
    for k, src, dst in along_row:
        def finish(d):
            relayed(k, dst, d).wait_recv()
            relay(k, dst, d).wait_send()
        finish(0)
        over(N // 2, finish)
        over(N // 2, lambda d: row_copy(k, src, dst, 2 * d).wait_send())
    for k, src, dst in along_wide:
        over(N, lambda d: wide_copy(k, src, dst, d).wait_send())


def gather(pieces):
    outs = [piece(p.dtype, N, *p.shape) for p in PIECES[:6]] + [piece(F32, 3, N, 24, PAIR)]
    return pl.pallas_call(
        gather_kernel,
        name="gather_panels",
        out_shape=outs,
        in_specs=[ANY] * 7,
        out_specs=[ANY] * 7,
        scratch_shapes=[
            pltpu.SemaphoreType.DMA((9, N)),
            pltpu.SemaphoreType.DMA((9, N)),
            pltpu.SemaphoreType.DMA((9,)),
            pltpu.SemaphoreType.DMA((19,)),
            pltpu.SemaphoreType.DMA((19,)),
        ],
        compiler_params=pltpu.CompilerParams(collective_id=0, has_side_effects=True),
    )(*pieces)


def dot(a, b):
    return jnp.dot(a, b, preferred_element_type=F32)


def split(a):
    high = a.astype(BF16)
    return high, (a - high.astype(F32)).astype(BF16)


def dot3(a, b):
    ah, al = split(a)
    bh, bl = split(b)
    return dot(ah, bh) + (dot(ah, bl) + dot(al, bh))


def invert(a_ref, out_ref, s_ref, x_ref, r_ref):
    n = PAIR
    eye = (
        lax.broadcasted_iota(jnp.int32, (n, n), 0) == lax.broadcasted_iota(jnp.int32, (n, n), 1)
    ).astype(F32)
    a = a_ref[...]
    across = lax.rsqrt(jnp.sum(a * eye, axis=0, keepdims=True))
    down = lax.rsqrt(jnp.sum(a * eye, axis=1, keepdims=True))
    s_ref[...] = a * across * down
    bound = jnp.max(jnp.sum(jnp.abs(s_ref[...]), axis=1, keepdims=True), axis=0, keepdims=True)
    start = 1.9 / bound
    x_ref[...] = start * eye
    r_ref[...] = eye - start * s_ref[...]

    def quick(_, c):
        r = r_ref[...].astype(BF16)
        x = x_ref[...]
        x_ref[...] = x + dot(x.astype(BF16), r)
        r_ref[...] = dot(r, r)
        return c

    lax.fori_loop(0, 6, quick, 0)

    def careful(state):
        step, _ = state
        r = eye - dot3(s_ref[...], x_ref[...])
        size = jnp.max(jnp.sum(jnp.abs(r), axis=1, keepdims=True))
        lost = jnp.logical_and(step == 0, jnp.logical_not(size < 0.9))
        r_ref[...] = r

        @pl.when(lost)
        def _():
            x_ref[...] = eye / bound

        @pl.when(jnp.logical_not(lost))
        def _():
            x = x_ref[...]
            x_ref[...] = x + dot3(x, r_ref[...])

        return step + 1, jnp.where(lost, 1.0, size)

    lax.while_loop(lambda s: jnp.logical_and(s[0] < 64, s[1] > 3e-4), careful, (0, 1.0))
    out_ref[...] = x_ref[...] * across * down


def factor_kernel(pv, ga, gb, t, s_ref, x_ref, r_ref, c_ref):
    invert(pv.at[0], ga, s_ref, x_ref, r_ref)
    cross = pv[1]
    t[...] = dot3(ga[...], cross)
    c_ref[...] = pv[2] - dot3(cross.T, t[...])
    invert(c_ref, gb, s_ref, x_ref, r_ref)


def factor(pv):
    block = piece(F32, PAIR, PAIR)
    return pl.pallas_call(
        factor_kernel,
        name="factor",
        out_shape=[block] * 3,
        in_specs=[VM],
        out_specs=[VM] * 3,
        scratch_shapes=[pltpu.VMEM((PAIR, PAIR), F32)] * 4,
    )(pv)


def per_device(hessian, weight, pairs):
    tile = hessian.shape[0]
    per_tile = tile // PAIR
    other = jnp.minimum(pairs[0], pairs[1])
    root = other // per_tile
    start = (other % per_tile) * PAIR
    last = (per_tile - 1) * PAIR

    cq = lax.dynamic_slice_in_dim(hessian, start, PAIR, 1)
    wq = lax.dynamic_slice_in_dim(weight, start, PAIR, 1)
    rq = lax.dynamic_slice_in_dim(hessian, start, PAIR, 0)
    pq = lax.dynamic_slice_in_dim(rq, start, PAIR, 1)
    c7 = hessian[:, last:]
    w7 = weight[:, last:]
    r7 = hessian[last:, :]
    operands = (
        cq.astype(BF16).reshape(N, 72, PAIR), wq.reshape(N, 18, PAIR), pq.reshape(N, 24, PAIR),
        rq.reshape(N, 24, tile), c7.astype(BF16).reshape(N, 72, PAIR), w7.reshape(N, 18, PAIR),
        r7.reshape(N, 24, tile),
    )
    pieces = lax.switch(root, [functools.partial(scatter, i) for i in range(N)], *operands)
    gcq, gwq, grq, gc7, gw7, gr7, gpv = gather(pieces)

    inv_a, inv_b, t = factor(gpv.reshape(3, PAIR, PAIR))
    high = lax.Precision.HIGH
    b0, b1 = grq.reshape(PAIR, tile), gr7.reshape(PAIR, tile)
    xa0 = jnp.dot(inv_a, b0, precision=high)
    rest = b1 - lax.dot_general(
        gpv.reshape(3, PAIR, PAIR)[1], xa0, (((0,), (0,)), ((), ())), precision=high
    )
    xb = jnp.dot(inv_b, rest, precision=high)
    xa = xa0 - jnp.dot(t, xb, precision=high)
    x = jnp.concatenate([xa, xb], 0)
    panel = jnp.concatenate([gcq.reshape(tile, PAIR), gc7.reshape(tile, PAIR)], 1)
    xh32 = lax.reduce_precision(x, 8, 7)
    xh, xl = xh32.astype(BF16), (x - xh32).astype(BF16)

    def pruned(axis, shape, dim):
        block = (lax.axis_index(axis) * tile + lax.broadcasted_iota(jnp.int32, shape, dim)) // PAIR
        return jnp.logical_or(block == other, block == NPAIRS - 1)

    gone = jnp.logical_or(pruned("row", (tile, 1), 0), pruned("wide", (1, tile), 1))
    pruned_hessian = jnp.where(gone, 0.0, hessian - dot(panel, xh))
    rows = weight.shape[0]
    wp = jnp.concatenate([gwq.reshape(rows, PAIR), gw7.reshape(rows, PAIR)], 1)
    pruned_weight = (weight.astype(F32) - (dot(wp, xh) + dot(wp, xl))).astype(BF16)
    return pruned_hessian, pruned_weight


def solution(mesh):
    return jax.shard_map(
        per_device,
        mesh=mesh,
        in_specs=(P("row", "wide"), P("row", "wide"), P()),
        out_specs=(P("row", "wide"), P("row", "wide")),
        check_vma=False,
    )
```

time: 925 us -> 175 us (0.19); the launches traced: 914 us -> 175 us
  waiting for transfers between devices: 607 us -> 0 us
  other arithmetic: 191 us -> 0.02 us
  Pallas kernels: 0 us -> 135 us
  matrix products: 60.4 us -> 17 us
  between operations: 19.5 us -> 2.21 us
  local copies, waits for them, and re-layouts: 36.2 us -> 20.5 us
    psum x5 -> x0, waiting for transfers between devices: 607 us -> none  [broadcast(): return lax.psum(kept, axis)]
    another operation x26 -> x0, other arithmetic: 176 us -> none  [the longest x21 115 us: solved_rows(): factor = jnp.linalg.cholesky(pivot_block)]
    pallas_call x0 -> x3, Pallas kernels: none -> 135 us  [the longest x1 89 us: gather(): pl.pallas_call(gather_kernel, name='gather_panels', out_shape=outs, in_sp...]
    another operation x28 -> x0, matrix products: 28.9 us -> none  [the longest x20 22.8 us: solved_rows(): solved = jax.scipy.linalg.cho_solve((factor, True), rows_local)]
    another operation x27 -> x0, local copies, waits for them, and re-layouts: 15.4 us -> none  [the longest x21 14.5 us: solved_rows(): solved = jax.scipy.linalg.cho_solve((factor, True), rows_local)]
    unnamed x18 -> x25, local copies, waits for them, and re-layouts: 17.1 us -> 1.7 us
    dot_general x4 -> x7, matrix products: 31.5 us -> 17 us  [the longest x3 8.48 us: dot(): return jnp.dot(a, b, preferred_element_type=F32)]
    select_n x8 -> x0, other arithmetic: 13.3 us -> none  [the longest x6 9.63 us: broadcast(): jnp.where(lax.axis_index(axis) == source, value, 0).astype(value.dtype)]
  transfers between devices with their start and end apart: 5 -> 0, of which waited for: 5 -> 0; matrix products, arithmetic and copies ran while one was open for 12% -> 0% of each run, Pallas kernels for 0% -> 0%
where the time goes in v1:
time: 175 us
  Pallas kernels  135 us (77%)
  local copies, waits for them, and re-layouts  20.5 us (12%)
  matrix products  17 us (10%)
  between operations  2.21 us (1%)
    pallas_call x1, Pallas kernels, gather(): pl.pallas_call(gather_kernel, name='gather_panels', out_shape=outs, in_sp...  89 us
    pallas_call x1, Pallas kernels, scatter(): pl.pallas_call(functools.partial(scatter_kernel, root), name=f'scatter_{r...  26.7 us
    pallas_call x1, Pallas kernels, factor(): pl.pallas_call(factor_kernel, name='factor', out_shape=[block] * 3, in_sp...  19.2 us
    dot_general x3, matrix products, dot(): return jnp.dot(a, b, preferred_element_type=F32)  8.48 us
    reshape x2, local copies, waits for them, and re-layouts, per_device(): wp = jnp.concatenate([gwq.reshape(rows, PAIR), gw7.reshape(rows, PAIR)], 1)  3.58 us
    slice x1, local copies, waits for them, and re-layouts, per_device(): c7 = hessian[:, last:]  3.51 us

profile of v1, /device:TPU:1, one launch (start us, length us, event | category | flops | bytes accessed | tf_op | source)
XLA Modules:
  0.0 175.0 jit_solution(11719787430224432982)
XLA Ops:
  0.6 1.3 fusion.18
  3.3 0.0 copy-start.5
  3.3 3.5 %fusion.16 = (bf16[1152,384]{1,0:T(8,128)(2,1)}, bf16[1152,384]{1,0:T(8,128)(2,1)}) fusion(f32[1152,1152]{1,0:T(8,128)} %param.19, s32[]{:T(128)S(6)} %select_n.47), kind=kLoop, calls=%fused_computation.38 | loop fusion | bytes 3538948 | tf_op jit(solution)/shard_map/slice | solution.py:371
  6.8 0.0 copy-done.5
  6.9 0.7 fusion.17
  7.6 0.8 reshape.105
  8.4 2.2 %dynamic_slice.14 = f32[384,384]{1,0:T(8,128)} dynamic-slice(f32[1152,1152]{1,0:T(8,128)} %param.19, s32[]{:T(128)S(6)} %select_n.48, s32[]{:T(128)S(6)} %select_n.48), dynamic_slice_sizes={384,384} | dynamic-slice | bytes 1179652 | tf_op jit(solution)/shard_map/dynamic_slice | solution.py:370
  10.5 2.2 %fusion.15 = (f32[384,1152]{1,0:T(8,128)S(1)}, f32[384,1152]{1,0:T(8,128)S(1)}) fusion(f32[1152,1152]{1,0:T(8,128)} %param.19, s32[]{:T(128)S(6)} %select_n.47), kind=kLoop, calls=%fused_computation.37 | loop fusion | bytes 7077892 | tf_op jit(solution)/shard_map/slice | solution.py:373
  12.8 1.7 reshape.109
  14.5 27.0 %conditional.1 = (bf16[72,384]{1,0:T(8,128)(2,1)}, bf16[18,384]{1,0:T(8,128)(2,1)}, f32[24,1152]{1,0:T(8,128)}, bf16[72,384]{1,0:T(8,128)(2,1)}, bf16[18,384]{1,...) conditional(s32[]{:T(128)} %clamp.7, ...), branch_computations={%region_0.1_spmd, %region_1.2_spmd, %region_2.3_spmd, %region_3.4_... | conditional | bytes 56 | solution.py:379
  14.5 26.7 %scatter_13.1 = (bf16[72,384]{1,0:T(8,128)(2,1)}, bf16[18,384]{1,0:T(8,128)(2,1)}, f32[24,1152]{1,0:T(8,128)}, bf16[72,384]{1,0:T(8,128)(2,1)}, bf16[18,384]{1,0...) custom-call(bf16[16,72,384]{2,1,0:T(8,128)(2,1)} %get-tuple-element.406.cq, ...), custom_call_target="tpu_custom_call" | custom-call | tf_op jit(solution)/shard_map/cond/branch_13_fun/scatter_13/pallas_call | solution.py:156
  41.5 89.0 %gather_panels.1 = (bf16[16,72,384]{2,1,0:T(8,128)(2,1)}, bf16[16,18,384]{2,1,0:T(8,128)(2,1)}, f32[16,24,1152]{2,1,0:T(8,128)}, bf16[16,72,384]{2,1,0:T(8,128)(...) custom-call(bf16[72,384]{1,0:T(8,128)(2,1)} %get-tuple-element.467.cq, ...), custom_call_target="tpu_custom_call" | custom-call | tf_op jit(solution)/shard_map/gather_panels/pallas_call | solution.py:262
  130.5 19.2 %factor.1 = (f32[384,384]{1,0:T(8,128)}, f32[384,384]{1,0:T(8,128)}, f32[384,384]{1,0:T(8,128)}) custom-call(f32[3,384,384]{2,1,0:T(8,128)} %bitcast.104), custom_call_target="tpu_custom_call" | custom-call | tf_op jit(solution)/shard_map/factor/pallas_call | solution.py:349
  149.7 1.1 slice.25
  150.8 0.0 copy-start
  150.9 3.4 %fusion.19 = f32[384,1152]{1,0:T(8,128)S(1)} fusion(f32[384,384]{1,0:T(8,128)} %get-tuple-element.477, f32[384,1152]{1,0:T(8,128)} %bitcast.107), kind=kOutput, calls=%fused_computation.41 | convolution fusion | flops 1019215872 | bytes 4128768 | tf_op jit(solution)/shard_map/dot_general | solution.py:385
  154.3 0.0 copy-done
  154.3 0.0 copy-start.4
  154.3 0.0 slice-start
  154.3 1.7 convolution_subtract_fusion.2
  156.0 0.0 copy-done.4
  156.1 0.0 copy-start.3
  156.1 0.0 slice-start.1
  156.1 1.7 fusion.20
  157.8 0.0 copy-done.3
  157.8 0.0 copy-start.8
  157.8 0.0 copy-start.9
  157.8 1.7 convolution_subtract_fusion.1
  159.5 0.0 slice-done
  159.6 0.0 slice-done.1
  159.6 0.0 copy-done.8
  159.6 0.0 copy-done.9
  159.6 0.0 copy-start.1
  159.6 5.0 %fusion = f32[1152,1152]{1,0:T(8,128)} fusion(f32[1152,1152]{1,0:T(8,128)S(1)} %bitcast.103, pred[1152]{0:T(1024)(128)(4,1)S(1)} %get-tuple-element.492, pred[1152]{0:T(1024)(128)(4,1)S(1)} %get-tuple-element.493, bf16[1152,384]{1,0:T(8,128)(2,1)S(1)} %bitcast.109, bf16[1152,384]{1,0:T(8,128)(2,1)S(1)} %bitcast.108, f32[384,1152]{1,0:T(8,128)S(1)} %fusion.20, ...), kind=kOutput, calls=%fused_computation.1 | convolution fusion | flops 2048606208 | bytes 15927552 | tf_op jit(solution)/shard_map/dot_general | solution.py:280
  164.6 0.0 copy-done.1
  164.6 0.0 copy-start.2
  164.6 1.9 %reshape.116 = bf16[288,384]{1,0:T(8,128)(2,1)} reshape(bf16[16,18,384]{2,1,0:T(8,128)(2,1)} %get-tuple-element.482) | data formatting | bytes 442368 | tf_op jit(solution)/shard_map/reshape | solution.py:403
  166.5 1.6 constant_dynamic-update-slice_fusion.1
  168.1 1.7 reshape.117
  169.8 1.6 constant_dynamic-update-slice_fusion
  171.5 0.0 copy-done.2
  171.5 0.0 copy-start.6
  171.5 0.0 copy-start.7
  171.5 1.8 %fusion.8 = f32[288,1152]{1,0:T(8,128)S(1)} fusion(bf16[288,768]{1,0:T(8,128)(2,1)} %constant_dynamic-update-slice_fusion, f32[384,1152]{1,0:T(8,128)S(1)} %fusion.20, f32[384,1152]{1,0:T(8,128)S(1)} %copy-done.2), kind=kOutput, calls=%fused_computation.16 | convolution fusion | flops 512262144 | bytes 5308416 | tf_op jit(solution)/shard_map/dot_general | solution.py:280
  173.3 0.0 copy-done.6
  173.3 0.0 copy-done.7
  173.3 1.6 fusion.3
  (2 shorter events, 0.0 us)
Async XLA Ops:
  3.3 3.5 %copy-start.5 = (bf16[288,1152]{1,0:T(8,128)(2,1)S(1)}, bf16[288,1152]{1,0:T(8,128)(2,1)}, u32[]{:S(2)}) copy-start(bf16[288,1152]{1,0:T(8,128)(2,1)} %param.20) | copy-start | bytes 1990660
  150.8 3.4 %copy-start = (f32[16,24,1152]{2,1,0:T(8,128)S(1)}, f32[16,24,1152]{2,1,0:T(8,128)}, u32[]{:S(2)}) copy-start(f32[16,24,1152]{2,1,0:T(8,128)} %get-tuple-element.481) | copy-start | bytes 5308420
  154.3 1.7 copy-start.4
  154.3 5.2 %slice-start = ((s8[5308416]{0:T(1024)(128)(4,1)}), s8[4194304]{0:T(1024)(128)(4,1)S(1)}, s32[]{:S(2)}) async-start(s8[5308416]{0:T(1024)(128)(4,1)} %bitcast.102), calls=%async_computation | async-start | bytes 8388608
  156.1 1.7 copy-start.3
  156.1 3.5 %slice-start.1 = ((s8[5308416]{0:T(1024)(128)(4,1)}), s8[1114112]{0:T(1024)(128)(4,1)S(1)}, s32[]{:S(2)}) async-start(s8[5308416]{0:T(1024)(128)(4,1)} %bitcast.102), calls=%async_computation.1 | async-start | bytes 2228224
  157.8 1.8 %copy-start.8 = (bf16[16,72,384]{2,1,0:T(8,128)(2,1)S(1)}, bf16[16,72,384]{2,1,0:T(8,128)(2,1)}, u32[]{:S(2)}) copy-start(bf16[16,72,384]{2,1,0:T(8,128)(2,1)} %get-tuple-element.474) | copy-start | bytes 2654212
  157.8 1.8 %copy-start.9 = (bf16[16,72,384]{2,1,0:T(8,128)(2,1)S(1)}, bf16[16,72,384]{2,1,0:T(8,128)(2,1)}, u32[]{:S(2)}) copy-start(bf16[16,72,384]{2,1,0:T(8,128)(2,1)} %get-tuple-element.475) | copy-start | bytes 2654212
  159.6 5.0 %copy-start.1 = (f32[384,1152]{1,0:T(8,128)}, f32[384,1152]{1,0:T(8,128)S(1)}, u32[]{:S(2)}) copy-start(f32[384,1152]{1,0:T(8,128)S(1)} %convolution_subtract_fusion.1) | copy-start | bytes 5308420
  164.6 6.9 %copy-start.2 = (f32[384,1152]{1,0:T(8,128)S(1)}, f32[384,1152]{1,0:T(8,128)}, u32[]{:S(2)}) copy-start(f32[384,1152]{1,0:T(8,128)} %copy-done.1) | copy-start | bytes 5308420
  171.5 1.9 %copy-start.6 = (bf16[288,1152]{1,0:T(8,128)(2,1)S(1)}, bf16[288,1152]{1,0:T(8,128)(2,1)}, u32[]{:S(2)}) copy-start(bf16[288,1152]{1,0:T(8,128)(2,1)} %param.20) | copy-start | bytes 1990660
  171.5 1.9 %copy-start.7 = (bf16[288,768]{1,0:T(8,128)(2,1)S(1)}, bf16[288,768]{1,0:T(8,128)(2,1)}, u32[]{:S(2)}) copy-start(bf16[288,768]{1,0:T(8,128)(2,1)} %constant_dynamic-update-slice_fusion) | copy-start | bytes 1327108

commit v2 on v1

--- a/solution.py
+++ b/solution.py
@@ -50,15 +50,15 @@
     at_wide, at_row = wide == root, row == root
     last_wide, last_row = wide == LAST, row == LAST
 
-    def corner(ref):
-        return lambda m: ref.at[m, :, pl.ds(2 * PAIR, PAIR)]
+    def strip(m, columns):
+        return r7.at[pl.ds(pl.multiple_of(2 * PAIR + 24 * m, 8), 24), columns]
 
     jobs = [
         (0, jnp.logical_and(at_row, at_wide), at_row, "wide", wide, lambda m: pq.at[m], pst.at[0]),
-        (1, jnp.logical_and(at_row, last_wide), at_row, "wide", wide, corner(rq), pst.at[1]),
-        (2, jnp.logical_and(last_row, last_wide), last_row, "wide", wide, corner(r7), pst.at[2]),
+        (1, jnp.logical_and(at_row, last_wide), at_row, "wide", wide, lambda m: rq.at[m, :, pl.ds(2 * PAIR, PAIR)], pst.at[1]),
+        (2, jnp.logical_and(last_row, last_wide), last_row, "wide", wide, lambda m: strip(m, pl.ds(2 * PAIR, PAIR)), pst.at[2]),
         (3, at_row, None, "row", row, lambda m: rq.at[m], orq),
-        (4, last_row, None, "row", row, lambda m: r7.at[m], or7),
+        (4, last_row, None, "row", row, lambda m: strip(m, slice(None)), or7),
         (5, at_wide, None, "wide", wide, lambda m: cq.at[m], ocq),
         (6, last_wide, None, "wide", wide, lambda m: c7.at[m], oc7),
         (7, at_wide, None, "wide", wide, lambda m: wq.at[m], owq),
@@ -169,92 +169,163 @@
 
 
 def gather_kernel(cq, wq, rq, c7, w7, r7, pv,
-                  gcq, gwq, grq, gc7, gw7, gr7, gpv, ssem, rsem, lsem, fsem, gsem):
+                  gcq, gwq, grq, gc7, gw7, gr7, gpv,
+                  lsem, xs, xr, zs, zr, hs, hr, ps, pr, fs, fr):
     row, wide = lax.axis_index("row"), lax.axis_index("wide")
-    core = lax.rem(row, 2)
-    greet_groups()
-    along_wide = [(0, cq, gcq), (1, c7, gc7), (2, wq, gwq), (3, w7, gw7)]
-    along_row = [(4, rq, grq), (5, r7, gr7)]
-    pivots = [(6, pv.at[0], gpv.at[0], 0), (7, pv.at[1], gpv.at[1], 0), (8, pv.at[2], gpv.at[2], 1)]
-
-    def wide_copy(k, src, dst, d):
-        return remote(src, dst.at[wide], ssem.at[k, d], rsem.at[k, d], {"wide": lax.rem(wide + d, N)})
-
-    def wide_arrival(k, src, dst, d):
-        return remote(src, dst.at[lax.rem(wide + N - d, N)], ssem.at[k, d], rsem.at[k, d],
-                      {"wide": lax.rem(wide + d, N)})
-
-    def row_copy(k, src, dst, d):
-        return remote(src, dst.at[row], ssem.at[k, d], rsem.at[k, d], {"row": lax.rem(row + d, N)})
-
-    def row_arrival(k, src, dst, d):
-        return remote(src, dst.at[lax.rem(row + N - d, N)], ssem.at[k, d], rsem.at[k, d],
-                      {"row": lax.rem(row + d, N)})
-
-    def over(n, f):
-        def body(d, _):
-            f(d)
-            return 0
-        lax.fori_loop(1, n, body, 0)
-
-    for k, src, dst, c in pivots:
-        @pl.when(core == c)
-        def _():
-            pltpu.make_async_copy(src, dst.at[wide], lsem.at[k]).start()
-            over(N, lambda d: wide_copy(k, src, dst, d).start())
-    for k, src, dst in along_row:
-        pltpu.make_async_copy(src, dst.at[row], lsem.at[k]).start()
-        over(N // 2, lambda d: row_copy(k, src, dst, 2 * d).start())
-    for k, src, dst in along_wide:
-        pltpu.make_async_copy(src, dst.at[wide], lsem.at[k]).start()
-        over(N, lambda d: wide_copy(k, src, dst, d).start())
-
-    partner = {"row": row + 1 - 2 * core}
-    for k, src, dst, c in pivots:
-        @pl.when(core == c)
-        def _():
-            pltpu.make_async_copy(src, dst.at[wide], lsem.at[k]).wait()
-            over(N, lambda d: wide_arrival(k, src, dst, d).wait_recv())
-            remote(dst, dst, fsem.at[k - 6], gsem.at[k - 6], partner).start()
-    for k, src, dst in along_row:
-        pltpu.make_async_copy(src, dst.at[row], lsem.at[k]).wait()
-
-    def relay(k, dst, d):
-        block = dst.at[lax.rem(row + N - 2 * d, N)]
-        return remote(block, block, fsem.at[3 + (k - 4) * 8 + d], gsem.at[3 + (k - 4) * 8 + d], partner)
-
-    def relayed(k, dst, d):
-        block = dst.at[lax.rem(row + 1 - 2 * core + N - 2 * d, N)]
-        return remote(block, block, fsem.at[3 + (k - 4) * 8 + d], gsem.at[3 + (k - 4) * 8 + d], partner)
-
-    for k, src, dst in along_row:
-        relay(k, dst, 0).start()
-
-        def step(d):
-            row_arrival(k, src, dst, 2 * d).wait_recv()
-            relay(k, dst, d).start()
-        over(N // 2, step)
-    for k, src, dst in along_wide:
-        pltpu.make_async_copy(src, dst.at[wide], lsem.at[k]).wait()
-        over(N, lambda d: wide_arrival(k, src, dst, d).wait_recv())
-    for k, src, dst, c in pivots:
-        @pl.when(core != c)
-        def _():
-            remote(dst, dst, fsem.at[k - 6], gsem.at[k - 6], partner).wait_recv()
-
-        @pl.when(core == c)
-        def _():
-            remote(dst, dst, fsem.at[k - 6], gsem.at[k - 6], partner).wait_send()
-            over(N, lambda d: wide_copy(k, src, dst, d).wait_send())
-    for k, src, dst in along_row:
-        def finish(d):
-            relayed(k, dst, d).wait_recv()
-            relay(k, dst, d).wait_send()
-        finish(0)
-        over(N // 2, finish)
-        over(N // 2, lambda d: row_copy(k, src, dst, 2 * d).wait_send())
-    for k, src, dst in along_wide:
-        over(N, lambda d: wide_copy(k, src, dst, d).wait_send())
+    core, x, upper = lax.rem(row, 2), lax.rem(row // 2, 4), row // 8
+    y, z = wide // 8, lax.rem(wide, 8)
+
+    def on_wide(t, dz):
+        return lax.rem(y + t, 2) * 8 + lax.rem(z + dz + 8, 8)
+
+    def on_row(t, dx, other=0):
+        chip = lax.rem(upper + t, 2) * 4 + lax.rem(x + dx + 4, 4)
+        return chip * 2 + (core if other == 0 else 1 - core)
+
+    neighbours = [
+        {"wide": on_wide(0, 1)}, {"wide": on_wide(0, -1)}, {"wide": on_wide(1, 0)},
+        {"row": on_row(0, 1)}, {"row": on_row(0, -1)}, {"row": on_row(1, 0)}, {"row": on_row(0, 0, 1)},
+    ]
+    barrier = pltpu.get_barrier_semaphore()
+    for where in neighbours:
+        pl.semaphore_signal(barrier, inc=1, device_id=where, device_id_type=MESH)
+    pl.semaphore_wait(barrier, len(neighbours))
+    partner = {"row": on_row(0, 0, 1)}
+
+    pivots = [(0, pv.at[0], gpv.at[0], 0, 0), (1, pv.at[1], gpv.at[1], 1, 0), (2, pv.at[2], gpv.at[2], 0, 1)]
+    columns = [(3, cq, gcq, 0, None), (4, c7, gc7, 1, None), (5, wq, gwq, 0, None), (6, w7, gw7, 1, None)]
+    rows = [(7, rq, grq, 0, None), (8, r7, gr7, 1, None)]
+    sign = (1, -1)
+
+    def only(job, f):
+        if job[4] is None:
+            f()
+        else:
+            pl.when(core == job[4])(f)
+
+    def local(job):
+        k, src, dst = job[:3]
+        return pltpu.make_async_copy(src, dst.at[row if k >= 7 else wide], lsem.at[k])
+
+    def across(job):
+        k, src, dst = job[:3]
+        if k >= 7:
+            return remote(src, dst.at[row], xs.at[k], xr.at[k], {"row": on_row(1, 0)})
+        return remote(src, dst.at[wide], xs.at[k], xr.at[k], {"wide": on_wide(1, 0)})
+
+    def crossed(job):
+        k, src, dst = job[:3]
+        if k >= 7:
+            return remote(src, dst.at[on_row(1, 0)], xs.at[k], xr.at[k], {"row": on_row(1, 0)})
+        return remote(src, dst.at[on_wide(1, 0)], xs.at[k], xr.at[k], {"wide": on_wide(1, 0)})
+
+    def hop(job, t, way, d, arriving=False):
+        k, src, dst = job[:3]
+        s = sign[way]
+        back = d if arriving else d - 1
+        if k >= 7:
+            block = dst.at[on_row(t, -s * back)]
+            start = src if isinstance(d, int) and d == 1 and t == 0 else block
+            return remote(start, block, hs.at[k - 7, t, way, d], hr.at[k - 7, t, way, d], {"row": on_row(0, s)})
+        block = dst.at[on_wide(t, -s * back)]
+        start = src if isinstance(d, int) and d == 1 and t == 0 else block
+        return remote(start, block, zs.at[k, t, way, d], zr.at[k, t, way, d], {"wide": on_wide(0, s)})
+
+    def share(job, t, dx, arriving=False):
+        k, src, dst = job[:3]
+        block = dst.at[on_row(t, dx, 1 if arriving else 0)]
+        rel = dx + 2
+        return remote(block, block, fs.at[k - 7, t, rel], fr.at[k - 7, t, rel], partner)
+
+    def begin(job):
+        local(job).start()
+        across(job).start()
+        hop(job, 0, 0, 1).start()
+        hop(job, 0, 1, 1).start()
+
+    def second(job):
+        crossed(job).wait_recv()
+        hop(job, 1, 0, 1).start()
+        hop(job, 1, 1, 1).start()
+
+    def pass_on(job, d, ways):
+        for t in (0, 1):
+            for way in (0, 1):
+                hop(job, t, way, d, True).wait_recv()
+                if ways == 2 or (ways == 1 and way == job[3]):
+                    hop(job, t, way, d + 1).start()
+
+    def last(job, d):
+        for t in (0, 1):
+            hop(job, t, job[3], d, True).wait_recv()
+
+    for job in pivots + rows + columns:
+        only(job, lambda: begin(job))
+    for job in rows:
+        local(job).wait()
+        share(job, 0, 0).start()
+    for job in pivots:
+        only(job, lambda: second(job))
+    for job in rows:
+        second(job)
+        share(job, 1, 0).start()
+    for job in columns:
+        second(job)
+
+    def middle(d, with_rows):
+        for job in pivots:
+            only(job, lambda: pass_on(job, d, 2 if d < 3 else 1))
+        if with_rows:
+            for job in rows:
+                if d == 1:
+                    pass_on(job, 1, 1)
+                    for t in (0, 1):
+                        share(job, t, -1).start()
+                        share(job, t, 1).start()
+                elif d == 2:
+                    last(job, 2)
+                    for t in (0, 1):
+                        share(job, t, -2).start()
+        for job in columns:
+            pass_on(job, d, 2 if d < 3 else 1)
+
+    for d in (1, 2, 3):
+        middle(d, d < 3)
+    for job in pivots:
+        def done(job=job):
+            local(job).wait()
+            last(job, 4)
+            remote(job[2], job[2], ps.at[job[0]], pr.at[job[0]], partner).start()
+        only(job, done)
+    for job in columns:
+        local(job).wait()
+        last(job, 4)
+
+    def sent(job):
+        across(job).wait_send()
+        full = 2 if job[0] >= 7 else 4
+        for t in (0, 1):
+            for way in (0, 1):
+                for d in range(1, full + 1 if way == job[3] else full):
+                    hop(job, t, way, d).wait_send()
+
+    for job in pivots:
+        def carried(job=job):
+            sent(job)
+            remote(job[2], job[2], ps.at[job[0]], pr.at[job[0]], partner).wait_send()
+        only(job, carried)
+
+        @pl.when(core != job[4])
+        def _():
+            remote(job[2], job[2], ps.at[job[0]], pr.at[job[0]], partner).wait_recv()
+    for job in columns:
+        sent(job)
+    for job in rows:
+        sent(job)
+        for t in (0, 1):
+            for dx in (0, -1, 1, -2):
+                share(job, t, dx, True).wait_recv()
+                share(job, t, dx).wait_send()
 
 
 def gather(pieces):
@@ -266,11 +337,17 @@
         in_specs=[ANY] * 7,
         out_specs=[ANY] * 7,
         scratch_shapes=[
-            pltpu.SemaphoreType.DMA((9, N)),
-            pltpu.SemaphoreType.DMA((9, N)),
             pltpu.SemaphoreType.DMA((9,)),
-            pltpu.SemaphoreType.DMA((19,)),
-            pltpu.SemaphoreType.DMA((19,)),
+            pltpu.SemaphoreType.DMA((9,)),
+            pltpu.SemaphoreType.DMA((9,)),
+            pltpu.SemaphoreType.DMA((7, 2, 2, 5)),
+            pltpu.SemaphoreType.DMA((7, 2, 2, 5)),
+            pltpu.SemaphoreType.DMA((2, 2, 2, 3)),
+            pltpu.SemaphoreType.DMA((2, 2, 2, 3)),
+            pltpu.SemaphoreType.DMA((3,)),
+            pltpu.SemaphoreType.DMA((3,)),
+            pltpu.SemaphoreType.DMA((2, 2, 4)),
+            pltpu.SemaphoreType.DMA((2, 2, 4)),
         ],
         compiler_params=pltpu.CompilerParams(collective_id=0, has_side_effects=True),
     )(*pieces)
@@ -356,26 +433,55 @@
     )(pv)
 
 
+def cut_kernel(block, hc, hr, hp, h7, wc, w7, ocq, owq, opq, orq, oc7, ow7):
+    for m in range(N // 2):
+        ocq[m] = hc[72 * m : 72 * m + 72, :].astype(BF16)
+        oc7[m] = h7[72 * m : 72 * m + 72, :].astype(BF16)
+        orq[m] = hr[24 * m : 24 * m + 24, :]
+        opq[m] = hp[24 * m : 24 * m + 24, :]
+    for src, out in ((wc, owq), (w7, ow7)):
+        full = src[...].astype(F32)
+        for m in range(N // 2):
+            out[m] = full[18 * m : 18 * m + 18, :].astype(BF16)
+
+
+def cut(block, hessian, weight):
+    half = N // 2
+
+    def out(*shape):
+        return pl.BlockSpec((half, *shape), lambda g, b: (g, 0, 0))
+
+    return pl.pallas_call(
+        cut_kernel,
+        name="cut",
+        out_shape=[
+            piece(BF16, N, 72, PAIR), piece(BF16, N, 18, PAIR), piece(F32, N, 24, PAIR),
+            piece(F32, N, 24, 1152), piece(BF16, N, 72, PAIR), piece(BF16, N, 18, PAIR),
+        ],
+        grid_spec=pltpu.PrefetchScalarGridSpec(
+            num_scalar_prefetch=1,
+            grid=(2,),
+            in_specs=[
+                pl.BlockSpec((576, PAIR), lambda g, b: (g, b[0])),
+                pl.BlockSpec((192, 1152), lambda g, b: (2 * b[0] + g, 0)),
+                pl.BlockSpec((192, PAIR), lambda g, b: (2 * b[0] + g, b[0])),
+                pl.BlockSpec((576, PAIR), lambda g, b: (g, 2)),
+                pl.BlockSpec((144, PAIR), lambda g, b: (g, b[0])),
+                pl.BlockSpec((144, PAIR), lambda g, b: (g, 2)),
+            ],
+            out_specs=[out(72, PAIR), out(18, PAIR), out(24, PAIR), out(24, 1152), out(72, PAIR), out(18, PAIR)],
+        ),
+    )(block, hessian, hessian, hessian, hessian, weight, weight)
+
+
 def per_device(hessian, weight, pairs):
     tile = hessian.shape[0]
     per_tile = tile // PAIR
     other = jnp.minimum(pairs[0], pairs[1])
     root = other // per_tile
-    start = (other % per_tile) * PAIR
-    last = (per_tile - 1) * PAIR
-
-    cq = lax.dynamic_slice_in_dim(hessian, start, PAIR, 1)
-    wq = lax.dynamic_slice_in_dim(weight, start, PAIR, 1)
-    rq = lax.dynamic_slice_in_dim(hessian, start, PAIR, 0)
-    pq = lax.dynamic_slice_in_dim(rq, start, PAIR, 1)
-    c7 = hessian[:, last:]
-    w7 = weight[:, last:]
-    r7 = hessian[last:, :]
-    operands = (
-        cq.astype(BF16).reshape(N, 72, PAIR), wq.reshape(N, 18, PAIR), pq.reshape(N, 24, PAIR),
-        rq.reshape(N, 24, tile), c7.astype(BF16).reshape(N, 72, PAIR), w7.reshape(N, 18, PAIR),
-        r7.reshape(N, 24, tile),
-    )
+    block = (other % per_tile).reshape(1)
+    cq, wq, pq, rq, c7, w7 = cut(block, hessian, weight)
+    operands = (cq, wq, pq, rq, c7, w7, hessian)
     pieces = lax.switch(root, [functools.partial(scatter, i) for i in range(N)], *operands)
     gcq, gwq, grq, gc7, gw7, gr7, gpv = gather(pieces)
 

time: 175 us -> 127 us (0.73)
  Pallas kernels: 135 us -> 99.9 us
  local copies, waits for them, and re-layouts: 20.5 us -> 9.18 us
    pallas_call x1, Pallas kernels: 89 us -> 52.7 us  [gather(): pl.pallas_call(gather_kernel, name='gather_panels', out_shape=outs, in_sp...]
    slice x3 -> x0, local copies, waits for them, and re-layouts: 6.48 us -> none  [the longest x1 3.51 us: per_device(): c7 = hessian[:, last:]]
    pallas_call x0 -> x1, Pallas kernels: none -> 4.03 us  [cut(): pl.pallas_call(cut_kernel, name='cut', out_shape=[piece(BF16, N, 72, PAIR...]
    pallas_call x1, Pallas kernels: 26.7 us -> 24 us  [scatter(): pl.pallas_call(functools.partial(scatter_kernel, root), name=f'scatter_{r...]
    reshape x2 -> x0, local copies, waits for them, and re-layouts: 2.53 us -> none  [the longest x1 1.75 us: per_device(): w7.reshape(N, 18, PAIR)]
    dynamic_slice x1 -> x0, local copies, waits for them, and re-layouts: 2.18 us -> none  [per_device(): pq = lax.dynamic_slice_in_dim(rq, start, PAIR, 1)]
where the time goes in v2:
time: 127 us; the launch traced here: 128 us
  Pallas kernels  99.9 us (79%)
  matrix products  16.5 us (13%)
  local copies, waits for them, and re-layouts  9.18 us (7%)
  between operations  2.2 us (2%)
    pallas_call x1, Pallas kernels, gather(): pl.pallas_call(gather_kernel, name='gather_panels', out_shape=outs, in_sp...  52.7 us
    pallas_call x1, Pallas kernels, scatter(): pl.pallas_call(functools.partial(scatter_kernel, root), name=f'scatter_{r...  24 us
    pallas_call x1, Pallas kernels, factor(): pl.pallas_call(factor_kernel, name='factor', out_shape=[block] * 3, in_sp...  19.3 us
    dot_general x3, matrix products, dot(): return jnp.dot(a, b, preferred_element_type=F32)  8.48 us
    pallas_call x1, Pallas kernels, cut(): pl.pallas_call(cut_kernel, name='cut', out_shape=[piece(BF16, N, 72, PAIR...  4.03 us
    reshape x2, local copies, waits for them, and re-layouts, per_device(): wp = jnp.concatenate([gwq.reshape(rows, PAIR), gw7.reshape(rows, PAIR)], 1)  3.43 us
    dot_general x1, matrix products, per_device(): xa0 = jnp.dot(inv_a, b0, precision=high)  2.88 us

profile of v2, /device:TPU:1, one launch (start us, length us, event | category | flops | bytes accessed | tf_op | source)
XLA Modules:
  0.0 128.1 jit_solution(12521934589190918785)
XLA Ops:
  0.6 1.3 %fusion.15 = (s32[1]{0:T(128)}, s32[1]{0:T(128)}) fusion(s32[2]{0:T(128)} %param.21), kind=kLoop, calls=%fused_computation.33 | loop fusion | bytes 16 | tf_op jit(solution)/shard_map/slice | solution.py:480
  3.3 4.0 %cut.1 = (bf16[16,72,384]{2,1,0:T(8,128)(2,1)S(1)}, bf16[16,18,384]{2,1,0:T(8,128)(2,1)}, f32[16,24,384]{2,1,0:T(8,128)}, f32[16,24,1152]{2,1,0:T(8,128)S(1)}, b...) custom-call(s32[1]{0:T(128)} %bitcast.1.block, f32[1152,1152]{1,0:T(8,128)} %h7.1, f32[1152,1152]{1,0:T(8,128)} %h7.1, ...), custom_call_target="tpu_custom_call" | custom-call | tf_op jit(solution)/shard_map/cut/pallas_call | solution.py:454
  7.3 24.2 %conditional.1 = (bf16[72,384]{1,0:T(8,128)(2,1)}, bf16[18,384]{1,0:T(8,128)(2,1)}, f32[24,1152]{1,0:T(8,128)}, bf16[72,384]{1,0:T(8,128)(2,1)}, bf16[18,384]{1,...) conditional(s32[]{:T(128)} %clamp.3, ...), branch_computations={%region_0.1_spmd, %region_1.2_spmd, %region_2.3_spmd, %region_3.4_... | conditional | bytes 56 | solution.py:485
  7.3 24.0 %scatter_3.1 = (bf16[72,384]{1,0:T(8,128)(2,1)}, bf16[18,384]{1,0:T(8,128)(2,1)}, f32[24,1152]{1,0:T(8,128)}, bf16[72,384]{1,0:T(8,128)(2,1)}, bf16[18,384]{1,0:...) custom-call(bf16[16,72,384]{2,1,0:T(8,128)(2,1)S(1)} %get-tuple-element.266.cq, ...), custom_call_target="tpu_custom_call" | custom-call | tf_op jit(solution)/shard_map/cond/branch_3_fun/scatter_3/pallas_call | solution.py:156
  31.5 52.7 %gather_panels.1 = (bf16[16,72,384]{2,1,0:T(8,128)(2,1)}, bf16[16,18,384]{2,1,0:T(8,128)(2,1)}, f32[16,24,1152]{2,1,0:T(8,128)}, bf16[16,72,384]{2,1,0:T(8,128)(...) custom-call(bf16[72,384]{1,0:T(8,128)(2,1)} %get-tuple-element.479.cq, ...), custom_call_target="tpu_custom_call" | custom-call | tf_op jit(solution)/shard_map/gather_panels/pallas_call | solution.py:333
  84.2 0.0 copy-start.2
  84.2 19.3 %factor.1 = (f32[384,384]{1,0:T(8,128)}, f32[384,384]{1,0:T(8,128)}, f32[384,384]{1,0:T(8,128)}) custom-call(f32[3,384,384]{2,1,0:T(8,128)} %bitcast.20), custom_call_target="tpu_custom_call" | custom-call | tf_op jit(solution)/shard_map/factor/pallas_call | solution.py:426
  103.5 1.1 slice.12
  104.6 0.0 copy-done.2
  104.6 0.0 copy-start.1
  104.6 2.9 %fusion.16 = f32[384,1152]{1,0:T(8,128)S(1)} fusion(f32[384,384]{1,0:T(8,128)} %get-tuple-element.489, f32[384,1152]{1,0:T(8,128)S(1)} %bitcast.23), kind=kOutput, calls=%fused_computation.34 | convolution fusion | flops 1019215872 | bytes 4128768 | tf_op jit(solution)/shard_map/dot_general | solution.py:491
  107.5 0.0 copy-done.1
  107.5 0.0 copy-start.4
  107.5 0.0 slice-start
  107.5 1.8 %convolution_subtract_fusion.2 = f32[384,1152]{1,0:T(8,128)S(1)} fusion(f32[384,1152]{1,0:T(8,128)S(1)} %bitcast.22, f32[384,384]{1,0:T(8,128)S(1)} %bitcast.21, f32[384,1152]{1,0:T(8,128)S(1)} %fusion.16), kind=kOutput, calls=%fused_computation.7 | convolution fusion | flops 1019658240 | bytes 5898240 | tf_op jit(solution)/shard_map/dot_general | solution.py:492
  109.3 0.0 copy-done.4
  109.3 0.0 copy-start.3
  109.3 0.0 slice-start.1
  109.3 1.7 %fusion.17 = f32[384,1152]{1,0:T(8,128)S(1)} fusion(f32[384,384]{1,0:T(8,128)S(1)} %copy-done.4, f32[384,1152]{1,0:T(8,128)S(1)} %convolution_subtract_fusion.2), kind=kOutput, calls=%fused_computation.35 | convolution fusion | flops 1019215872 | bytes 4128768 | tf_op jit(solution)/shard_map/dot_general | solution.py:495
  111.0 0.0 copy-done.3
  111.1 0.0 copy-start.6
  111.1 0.0 copy-start.7
  111.1 1.7 %convolution_subtract_fusion.1 = f32[384,1152]{1,0:T(8,128)S(1)} fusion(f32[384,1152]{1,0:T(8,128)S(1)} %fusion.16, f32[384,384]{1,0:T(8,128)S(1)} %copy-done.3, f32[384,1152]{1,0:T(8,128)S(1)} %fusion.17), kind=kOutput, calls=%fused_computation.6 | convolution fusion | flops 1019658240 | bytes 5898240 | tf_op jit(solution)/shard_map/dot_general | solution.py:496
  112.8 0.0 slice-done
  112.8 0.0 slice-done.1
  112.8 0.0 copy-done.6
  112.8 0.0 copy-done.7
  112.8 5.0 %fusion = f32[1152,1152]{1,0:T(8,128)} fusion(f32[1152,1152]{1,0:T(8,128)S(1)} %bitcast.19, pred[1152]{0:T(1024)(128)(4,1)S(1)} %get-tuple-element.498, pred[1152]{0:T(1024)(128)(4,1)S(1)} %get-tuple-element.499, bf16[1152,384]{1,0:T(8,128)(2,1)S(1)} %bitcast.25, bf16[1152,384]{1,0:T(8,128)(2,1)S(1)} %bitcast.24, f32[384,1152]{1,0:T(8,128)S(1)} %fusion.17, ...), kind=kOutput, calls=%fused_computation.1 | convolution fusion | flops 2048606208 | bytes 15927552 | tf_op jit(solution)/shard_map/dot_general | solution.py:357
  117.8 1.7 %reshape.92 = bf16[288,384]{1,0:T(8,128)(2,1)} reshape(bf16[16,18,384]{2,1,0:T(8,128)(2,1)} %get-tuple-element.494) | data formatting | bytes 442368 | tf_op jit(solution)/shard_map/reshape | solution.py:509
  119.6 1.6 %constant_dynamic-update-slice_fusion.1 = bf16[288,768]{1,0:T(8,128)(2,1)} fusion(bf16[288,384]{1,0:T(8,128)(2,1)} %reshape.92), kind=kLoop, calls=%fused_computation.28 | loop fusion | bytes 442368
  121.2 1.7 %reshape.93 = bf16[288,384]{1,0:T(8,128)(2,1)} reshape(bf16[16,18,384]{2,1,0:T(8,128)(2,1)} %get-tuple-element.495) | data formatting | bytes 442368 | tf_op jit(solution)/shard_map/reshape | solution.py:509
  122.9 1.6 %constant_dynamic-update-slice_fusion = bf16[288,768]{1,0:T(8,128)(2,1)} fusion(bf16[288,768]{1,0:T(8,128)(2,1)} %constant_dynamic-update-slice_fusion.1, bf16[288,384]{1,0:T(8,128)(2,1)} %reshape.93), kind=kLoop, calls=%fused_computation.27 | loop fusion | bytes 442368 | tf_op jit(solution)/shard_map/concatenate | solution.py:509
  124.6 0.0 copy-start
  124.6 0.0 copy-start.5
  124.6 1.8 %fusion.8 = f32[288,1152]{1,0:T(8,128)S(1)} fusion(bf16[288,768]{1,0:T(8,128)(2,1)} %constant_dynamic-update-slice_fusion, f32[384,1152]{1,0:T(8,128)S(1)} %fusion.17, f32[384,1152]{1,0:T(8,128)S(1)} %convolution_subtract_fusion.1), kind=kOutput, calls=%fused_computation.14 | convolution fusion | flops 512262144 | bytes 5308416 | tf_op jit(solution)/shard_map/dot_general | solution.py:357
  126.4 0.0 copy-done
  126.4 0.0 copy-done.5
  126.4 1.6 %fusion.3 = bf16[288,1152]{1,0:T(8,128)(2,1)} fusion(f32[288,1152]{1,0:T(8,128)S(1)} %fusion.8, bf16[288,768]{1,0:T(8,128)(2,1)S(1)} %copy-done.5, f32[384,1152]{1,0:T(8,128)S(1)} %fusion.17, f32[384,1152]{1,0:T(8,128)S(1)} %convolution_subtract_fusion.1, bf16[288,1152]{1,0:T(8,128)(2,1)S(1)} %copy-done), kind=kOutput, calls=%fused_computation.10 | convolution fusion | flops 514473984 | bytes 6635520 | tf_op jit(solution)/shard_map/dot_general | solution.py:357
  (2 shorter events, 0.0 us)
Async XLA Ops:
  84.2 20.4 %copy-start.2 = (f32[16,24,1152]{2,1,0:T(8,128)S(1)}, f32[16,24,1152]{2,1,0:T(8,128)}, u32[]{:S(2)}) copy-start(f32[16,24,1152]{2,1,0:T(8,128)} %get-tuple-element.490) | copy-start | bytes 5308420
  104.6 2.9 %copy-start.1 = (f32[16,24,1152]{2,1,0:T(8,128)S(1)}, f32[16,24,1152]{2,1,0:T(8,128)}, u32[]{:S(2)}) copy-start(f32[16,24,1152]{2,1,0:T(8,128)} %get-tuple-element.493) | copy-start | bytes 5308420
  107.5 1.8 %copy-start.4 = (f32[384,384]{1,0:T(8,128)S(1)}, f32[384,384]{1,0:T(8,128)}, u32[]{:S(2)}) copy-start(f32[384,384]{1,0:T(8,128)} %get-tuple-element.492) | copy-start | bytes 1769476
  107.5 5.3 %slice-start = ((s8[5308416]{0:T(1024)(128)(4,1)}), s8[4194304]{0:T(1024)(128)(4,1)S(1)}, s32[]{:S(2)}) async-start(s8[5308416]{0:T(1024)(128)(4,1)} %bitcast.18), calls=%async_computation | async-start | bytes 8388608
  109.3 1.7 %copy-start.3 = (f32[384,384]{1,0:T(8,128)S(1)}, f32[384,384]{1,0:T(8,128)}, u32[]{:S(2)}) copy-start(f32[384,384]{1,0:T(8,128)} %get-tuple-element.491) | copy-start | bytes 1769476
  109.3 3.5 %slice-start.1 = ((s8[5308416]{0:T(1024)(128)(4,1)}), s8[1114112]{0:T(1024)(128)(4,1)S(1)}, s32[]{:S(2)}) async-start(s8[5308416]{0:T(1024)(128)(4,1)} %bitcast.18), calls=%async_computation.1 | async-start | bytes 2228224
  111.1 1.8 %copy-start.6 = (bf16[16,72,384]{2,1,0:T(8,128)(2,1)S(1)}, bf16[16,72,384]{2,1,0:T(8,128)(2,1)}, u32[]{:S(2)}) copy-start(bf16[16,72,384]{2,1,0:T(8,128)(2,1)} %get-tuple-element.486) | copy-start | bytes 2654212
  111.1 1.8 %copy-start.7 = (bf16[16,72,384]{2,1,0:T(8,128)(2,1)S(1)}, bf16[16,72,384]{2,1,0:T(8,128)(2,1)}, u32[]{:S(2)}) copy-start(bf16[16,72,384]{2,1,0:T(8,128)(2,1)} %get-tuple-element.487) | copy-start | bytes 2654212
  124.6 1.9 %copy-start = (bf16[288,1152]{1,0:T(8,128)(2,1)S(1)}, bf16[288,1152]{1,0:T(8,128)(2,1)}, u32[]{:S(2)}) copy-start(bf16[288,1152]{1,0:T(8,128)(2,1)} %w7.1) | copy-start | bytes 1990660
  124.6 1.9 %copy-start.5 = (bf16[288,768]{1,0:T(8,128)(2,1)S(1)}, bf16[288,768]{1,0:T(8,128)(2,1)}, u32[]{:S(2)}) copy-start(bf16[288,768]{1,0:T(8,128)(2,1)} %constant_dynamic-update-slice_fusion) | copy-start | bytes 1327108

commit v3 on v2

--- a/solution.py
+++ b/solution.py
@@ -259,44 +259,37 @@
         for t in (0, 1):
             hop(job, t, job[3], d, True).wait_recv()
 
-    for job in pivots + rows + columns:
+    for job in pivots + columns + rows:
         only(job, lambda: begin(job))
+    for job in pivots + columns:
+        only(job, lambda: second(job))
     for job in rows:
         local(job).wait()
         share(job, 0, 0).start()
-    for job in pivots:
-        only(job, lambda: second(job))
+    for job in pivots + columns:
+        only(job, lambda: pass_on(job, 1, 2))
     for job in rows:
         second(job)
         share(job, 1, 0).start()
-    for job in columns:
-        second(job)
-
-    def middle(d, with_rows):
-        for job in pivots:
-            only(job, lambda: pass_on(job, d, 2 if d < 3 else 1))
-        if with_rows:
-            for job in rows:
-                if d == 1:
-                    pass_on(job, 1, 1)
-                    for t in (0, 1):
-                        share(job, t, -1).start()
-                        share(job, t, 1).start()
-                elif d == 2:
-                    last(job, 2)
-                    for t in (0, 1):
-                        share(job, t, -2).start()
-        for job in columns:
-            pass_on(job, d, 2 if d < 3 else 1)
-
-    for d in (1, 2, 3):
-        middle(d, d < 3)
+    for job in pivots + columns:
+        only(job, lambda: pass_on(job, 2, 2))
+    for job in rows:
+        pass_on(job, 1, 1)
+        for t in (0, 1):
+            share(job, t, -1).start()
+            share(job, t, 1).start()
+    for job in pivots + columns:
+        only(job, lambda: pass_on(job, 3, 1))
     for job in pivots:
         def done(job=job):
             local(job).wait()
             last(job, 4)
             remote(job[2], job[2], ps.at[job[0]], pr.at[job[0]], partner).start()
         only(job, done)
+    for job in rows:
+        last(job, 2)
+        for t in (0, 1):
+            share(job, t, -2).start()
     for job in columns:
         local(job).wait()
         last(job, 4)
@@ -376,61 +369,164 @@
     a = a_ref[...]
     across = lax.rsqrt(jnp.sum(a * eye, axis=0, keepdims=True))
     down = lax.rsqrt(jnp.sum(a * eye, axis=1, keepdims=True))
-    s_ref[...] = a * across * down
-    bound = jnp.max(jnp.sum(jnp.abs(s_ref[...]), axis=1, keepdims=True), axis=0, keepdims=True)
+    s = a * across * down
+    s_ref[0], s_ref[1] = split(s)
+    bound = jnp.max(jnp.sum(jnp.abs(s), axis=1, keepdims=True), axis=0, keepdims=True)
     start = 1.9 / bound
     x_ref[...] = start * eye
-    r_ref[...] = eye - start * s_ref[...]
+    r_ref[...] = eye - start * s
 
     def quick(_, c):
         r = r_ref[...].astype(BF16)
         x = x_ref[...]
-        x_ref[...] = x + dot(x.astype(BF16), r)
-        r_ref[...] = dot(r, r)
+        both = dot(jnp.concatenate([x.astype(BF16), r], 0), r)
+        x_ref[...] = x + both[:n]
+        r_ref[...] = both[n:]
         return c
 
-    lax.fori_loop(0, 6, quick, 0)
+    lax.fori_loop(0, 5, quick, 0)
 
     def careful(state):
         step, _ = state
-        r = eye - dot3(s_ref[...], x_ref[...])
+        xh, xl = split(x_ref[...])
+        r = eye - (dot(s_ref[0], xh) + (dot(s_ref[0], xl) + dot(s_ref[1], xh)))
         size = jnp.max(jnp.sum(jnp.abs(r), axis=1, keepdims=True))
         lost = jnp.logical_and(step == 0, jnp.logical_not(size < 0.9))
+        near = size < 0.25
         r_ref[...] = r
 
         @pl.when(lost)
         def _():
             x_ref[...] = eye / bound
 
-        @pl.when(jnp.logical_not(lost))
+        @pl.when(jnp.logical_and(jnp.logical_not(lost), jnp.logical_not(near)))
+        def _():
+            x_ref[...] = x_ref[...] + dot3(x_ref[...], r_ref[...])
+
+        @pl.when(near)
         def _():
             x = x_ref[...]
-            x_ref[...] = x + dot3(x, r_ref[...])
+            x_ref[...] = x + dot(x.astype(BF16), r_ref[...].astype(BF16))
 
         return step + 1, jnp.where(lost, 1.0, size)
 
-    lax.while_loop(lambda s: jnp.logical_and(s[0] < 64, s[1] > 3e-4), careful, (0, 1.0))
+    lax.while_loop(lambda s: jnp.logical_and(s[0] < 64, s[1] > 1e-3), careful, (0, 1.0))
     out_ref[...] = x_ref[...] * across * down
 
 
-def factor_kernel(pv, ga, gb, t, s_ref, x_ref, r_ref, c_ref):
-    invert(pv.at[0], ga, s_ref, x_ref, r_ref)
-    cross = pv[1]
-    t[...] = dot3(ga[...], cross)
-    c_ref[...] = pv[2] - dot3(cross.T, t[...])
-    invert(c_ref, gb, s_ref, x_ref, r_ref)
-
-
-def factor(pv):
-    block = piece(F32, PAIR, PAIR)
+def finish_kernel(other, pv, b0, b1, cq, c7, wq, w7, h, w, oh, ow,
+                  s_ref, x_ref, r_ref, g_ref, c_ref, m_ref, b_ref, xh_ref, xl_ref, w_ref, sem):
+    step = pl.program_id(0)
+    tiles = 1152 // PAIR
+
+    def over_tiles(f):
+        def body(j, c):
+            f(pl.ds(pl.multiple_of(j * PAIR, PAIR), PAIR))
+            return c
+        lax.fori_loop(0, tiles, body, 0)
+
+    @pl.when(step == 0)
+    def _():
+        loads = [pltpu.make_async_copy(b, b_ref.at[i], sem.at[i]) for i, b in enumerate((b0, b1))]
+        for load in loads:
+            load.start()
+
+        def keep(i, value):
+            m_ref[i, 0], m_ref[i, 1] = split(value)
+
+        def times(i, value):
+            high, low = split(value)
+            return dot(m_ref[i, 0], high) + (dot(m_ref[i, 0], low) + dot(m_ref[i, 1], high))
+
+        invert(pv.at[0], g_ref, s_ref, x_ref, r_ref)
+        keep(0, g_ref[...])
+        keep(1, pv[1].T)
+        t = times(0, pv[1])
+        keep(3, t)
+        c_ref[...] = pv[2] - times(1, t)
+        invert(c_ref, g_ref, s_ref, x_ref, r_ref)
+        keep(2, g_ref[...])
+        for i, panel in enumerate((wq, w7)):
+            for m in range(N):
+                w_ref[i, 18 * m : 18 * m + 18, :] = panel[m].astype(F32)
+        for load in loads:
+            load.wait()
+
+        def solve(cols):
+            first = times(0, b_ref[0, :, cols])
+            xb = times(2, b_ref[1, :, cols] - times(1, first))
+            xa = first - times(3, xb)
+            ah, al = split(xa)
+            bh, bl = split(xb)
+            xh_ref[0, :, cols], xl_ref[0, :, cols] = ah, al
+            xh_ref[1, :, cols], xl_ref[1, :, cols] = bh, bl
+            p0, p1 = w_ref[0].astype(BF16), w_ref[1].astype(BF16)
+            change = (dot(p0, ah) + dot(p1, bh)) + (dot(p0, al) + dot(p1, bl))
+            ow[:, cols] = (w[:, cols].astype(F32) - change).astype(BF16)
+
+        over_tiles(solve)
+
+    strip = h.shape[0]
+
+    def pruned(origin, shape, dim):
+        place = lax.broadcasted_iota(jnp.int32, shape, dim) + origin
+        begin = other[0] * PAIR
+        return jnp.logical_or(
+            jnp.logical_and(place >= begin, place < begin + PAIR), place >= (NPAIRS - 1) * PAIR
+        )
+
+    lines = lax.axis_index("row") * 1152 + step * strip
+
+    def update(j, c):
+        cols = pl.ds(pl.multiple_of(j * PAIR, PAIR), PAIR)
+        gone = jnp.logical_or(
+            pruned(lines, (strip, PAIR), 0),
+            pruned(lax.axis_index("wide") * 1152 + j * PAIR, (strip, PAIR), 1),
+        )
+        change = dot(cq[...], xh_ref[0, :, cols]) + dot(c7[...], xh_ref[1, :, cols])
+        oh[:, cols] = jnp.where(gone, 0.0, h[:, cols] - change)
+        return c
+
+    lax.fori_loop(0, tiles, update, 0)
+
+
+def finish(other, pv, b0, b1, cq, c7, wq, w7, hessian, weight):
+    steps = 4
+    strip = 1152 // steps
+
+    def whole(*shape):
+        return pl.BlockSpec(shape, lambda g, o: (0,) * len(shape))
+
+    def strips(columns):
+        return pl.BlockSpec((strip, columns), lambda g, o: (g, 0))
+
     return pl.pallas_call(
-        factor_kernel,
-        name="factor",
-        out_shape=[block] * 3,
-        in_specs=[VM],
-        out_specs=[VM] * 3,
-        scratch_shapes=[pltpu.VMEM((PAIR, PAIR), F32)] * 4,
-    )(pv)
+        finish_kernel,
+        name="finish",
+        out_shape=[piece(F32, 1152, 1152), piece(BF16, 288, 1152)],
+        grid_spec=pltpu.PrefetchScalarGridSpec(
+            num_scalar_prefetch=1,
+            grid=(steps,),
+            in_specs=[
+                whole(3, PAIR, PAIR), ANY, ANY, strips(PAIR), strips(PAIR),
+                whole(N, 18, PAIR), whole(N, 18, PAIR), strips(1152), whole(288, 1152),
+            ],
+            out_specs=[strips(1152), whole(288, 1152)],
+            scratch_shapes=[
+                pltpu.VMEM((2, PAIR, PAIR), BF16),
+                pltpu.VMEM((PAIR, PAIR), F32),
+                pltpu.VMEM((PAIR, PAIR), F32),
+                pltpu.VMEM((PAIR, PAIR), F32),
+                pltpu.VMEM((PAIR, PAIR), F32),
+                pltpu.VMEM((4, 2, PAIR, PAIR), BF16),
+                pltpu.VMEM((2, PAIR, 1152), F32),
+                pltpu.VMEM((2, PAIR, 1152), BF16),
+                pltpu.VMEM((2, PAIR, 1152), BF16),
+                pltpu.VMEM((2, 288, PAIR), F32),
+                pltpu.SemaphoreType.DMA((2,)),
+            ],
+        ),
+    )(other, pv, b0, b1, cq, c7, wq, w7, hessian, weight)
 
 
 def cut_kernel(block, hc, hr, hp, h7, wc, w7, ocq, owq, opq, orq, oc7, ow7):
@@ -485,30 +581,10 @@
     pieces = lax.switch(root, [functools.partial(scatter, i) for i in range(N)], *operands)
     gcq, gwq, grq, gc7, gw7, gr7, gpv = gather(pieces)
 
-    inv_a, inv_b, t = factor(gpv.reshape(3, PAIR, PAIR))
-    high = lax.Precision.HIGH
-    b0, b1 = grq.reshape(PAIR, tile), gr7.reshape(PAIR, tile)
-    xa0 = jnp.dot(inv_a, b0, precision=high)
-    rest = b1 - lax.dot_general(
-        gpv.reshape(3, PAIR, PAIR)[1], xa0, (((0,), (0,)), ((), ())), precision=high
+    return finish(
+        other.reshape(1), gpv.reshape(3, PAIR, PAIR), grq.reshape(PAIR, tile), gr7.reshape(PAIR, tile),
+        gcq.reshape(tile, PAIR), gc7.reshape(tile, PAIR), gwq, gw7, hessian, weight,
     )
-    xb = jnp.dot(inv_b, rest, precision=high)
-    xa = xa0 - jnp.dot(t, xb, precision=high)
-    x = jnp.concatenate([xa, xb], 0)
-    panel = jnp.concatenate([gcq.reshape(tile, PAIR), gc7.reshape(tile, PAIR)], 1)
-    xh32 = lax.reduce_precision(x, 8, 7)
-    xh, xl = xh32.astype(BF16), (x - xh32).astype(BF16)
-
-    def pruned(axis, shape, dim):
-        block = (lax.axis_index(axis) * tile + lax.broadcasted_iota(jnp.int32, shape, dim)) // PAIR
-        return jnp.logical_or(block == other, block == NPAIRS - 1)
-
-    gone = jnp.logical_or(pruned("row", (tile, 1), 0), pruned("wide", (1, tile), 1))
-    pruned_hessian = jnp.where(gone, 0.0, hessian - dot(panel, xh))
-    rows = weight.shape[0]
-    wp = jnp.concatenate([gwq.reshape(rows, PAIR), gw7.reshape(rows, PAIR)], 1)
-    pruned_weight = (weight.astype(F32) - (dot(wp, xh) + dot(wp, xl))).astype(BF16)
-    return pruned_hessian, pruned_weight
 
 
 def solution(mesh):

time: 127 us -> 115 us (0.906)
  the two profiles are of different devices: /device:TPU:1 before, /device:TPU:25 now
where the time goes in v3:
time: 115 us; the launch traced here: 113 us
  Pallas kernels  109 us (95%)
  between operations  2.14 us (2%)
  local copies, waits for them, and re-layouts  1.31 us (1%)
    pallas_call x1, Pallas kernels, gather(): pl.pallas_call(gather_kernel, name='gather_panels', out_shape=outs, in_sp...  51.3 us
    pallas_call x1, Pallas kernels, finish(): pl.pallas_call(finish_kernel, name='finish', out_shape=[piece(F32, 1152,...  33.2 us
    pallas_call x1, Pallas kernels, scatter(): pl.pallas_call(functools.partial(scatter_kernel, root), name=f'scatter_{r...  20.9 us
    pallas_call x1, Pallas kernels, cut(): pl.pallas_call(cut_kernel, name='cut', out_shape=[piece(BF16, N, 72, PAIR...  3.78 us

profile of v3, /device:TPU:25, one launch (start us, length us, event | category | flops | bytes accessed | tf_op | source)
XLA Modules:
  0.0 112.9 jit_solution(6365867750272052166)
XLA Ops:
  0.6 1.3 %fusion = (s32[1]{0:T(128)}, s32[1]{0:T(128)}) fusion(s32[2]{0:T(128)} %param.21), kind=kLoop, calls=%fused_computation | loop fusion | bytes 16 | tf_op jit(solution)/shard_map/slice | solution.py:576
  3.3 3.8 %cut.1 = (bf16[16,72,384]{2,1,0:T(8,128)(2,1)S(1)}, bf16[16,18,384]{2,1,0:T(8,128)(2,1)}, f32[16,24,384]{2,1,0:T(8,128)}, f32[16,24,1152]{2,1,0:T(8,128)S(1)}, b...) custom-call(s32[1]{0:T(128)} %bitcast.3.block, f32[1152,1152]{1,0:T(8,128)} %h.1, f32[1152,1152]{1,0:T(8,128)} %h.1, ...), custom_call_target="tpu_custom_call" | custom-call | tf_op jit(solution)/shard_map/cut/pallas_call | solution.py:550
  7.1 21.1 %conditional.1 = (bf16[72,384]{1,0:T(8,128)(2,1)}, bf16[18,384]{1,0:T(8,128)(2,1)}, f32[24,1152]{1,0:T(8,128)}, bf16[72,384]{1,0:T(8,128)(2,1)}, bf16[18,384]{1,...) conditional(s32[]{:T(128)} %clamp.3, ...), branch_computations={%region_0.1_spmd, %region_1.2_spmd, %region_2.3_spmd, %region_3.4_... | conditional | bytes 56 | solution.py:581
  7.1 20.9 %scatter_2.1 = (bf16[72,384]{1,0:T(8,128)(2,1)}, bf16[18,384]{1,0:T(8,128)(2,1)}, f32[24,1152]{1,0:T(8,128)}, bf16[72,384]{1,0:T(8,128)(2,1)}, bf16[18,384]{1,0:...) custom-call(bf16[16,72,384]{2,1,0:T(8,128)(2,1)S(1)} %get-tuple-element.252.cq, ...), custom_call_target="tpu_custom_call" | custom-call | tf_op jit(solution)/shard_map/cond/branch_2_fun/scatter_2/pallas_call | solution.py:156
  28.2 51.3 %gather_panels.1 = (bf16[16,72,384]{2,1,0:T(8,128)(2,1)}, bf16[16,18,384]{2,1,0:T(8,128)(2,1)}, f32[16,24,1152]{2,1,0:T(8,128)}, bf16[16,72,384]{2,1,0:T(8,128)(...) custom-call(bf16[72,384]{1,0:T(8,128)(2,1)} %get-tuple-element.476.cq, ...), custom_call_target="tpu_custom_call" | custom-call | tf_op jit(solution)/shard_map/gather_panels/pallas_call | solution.py:326
  79.5 33.2 %finish.1 = (f32[1152,1152]{1,0:T(8,128)}, bf16[288,1152]{1,0:T(8,128)(2,1)}) custom-call(s32[1]{0:T(128)S(6)} %min.4.other, f32[3,384,384]{2,1,0:T(8,128)} %bitcast.11, f32[384,1152]{1,0:T(8,128)} %bitcast.9, f32[384,1152]{1,0:T(8,128)} %bitcast.10, bf16[1152,384]{1,0:T(8,128)(2,1)} %bitcast.12, bf16[1152,384]{1,0:T(8,128)(2,1)} %bitcast.13, ...), custom_call_target="tpu_custom_call" | custom-call | tf_op jit(solution)/shard_map/finish/pallas_call | solution.py:503
